TPU v7x, 32 devices: a whole 2x2x4 slice. The times are simulated.
32 devices in a mesh: section: 4 (over z), ctx: 8 (over y, x, core).
Axes of the slice: x: 2, y: 2, z: 4, core: 2. Of those that a mesh axis runs over, the one named last changes fastest.
Arguments:
- gate_rows: bfloat16 [4, 1024, 4096], P('section', 'ctx'), may hold values from -6 to 6
- key_rows: bfloat16 [4, 1024, 4096], P('section', 'ctx'), may hold values from -6 to 6
- value_rows: bfloat16 [4, 1024, 4096], P('section', 'ctx'), may hold values from -6 to 6
- filters: bfloat16 [4, 1024, 256], P('section', 'ctx'), may hold values from -1.1 to 1.1
- skip_gain: float32 [4096], replicated, may hold values from -3 to 3
Outputs:
- passed: bfloat16 [4, 1024, 4096], P('section', 'ctx')
All inputs are finite; a program needn't handle non-finite values.
Results may differ from a plain program's by a relative error of at most 0.007.
Values may be sent and summed in bfloat16 or wider, within the bound.
A program may use at most 64 MiB of HBM per device.

v0:
```python
import functools

import jax
import jax.numpy as jnp
from jax import lax
from jax.experimental import pallas as pl
from jax.experimental.pallas import tpu as pltpu
from jax.sharding import PartitionSpec as P

MESH = pl.DeviceIdType.MESH
LANES = 128


def kernel(
    n, sections, taps,
    gate_hbm, key_hbm, value_hbm, filt_hbm, skip_ref, out_hbm,
    gate_v, key_v, value_v, filt_v, turned, send_rows, taps_send, got_rows, got_taps,
    conv_send, conv_got, gated, acc_ref,
    load_sem, rows_ssem, rows_rsem, taps_ssem, taps_rsem,
    back_ssem, back_rsem, pass_ssem, pass_rsem, own_sem,
):
    rows = key_v.shape[0]
    groups = filt_v.shape[1]
    depth = key_v.shape[1] // groups
    halves = groups // LANES
    per = LANES // n
    me = lax.axis_index("ctx")
    sec = lax.axis_index("section")
    after = lax.rem(sec + 1, sections)
    before = lax.rem(sec + sections - 1, sections)

    loads = [
        pltpu.make_async_copy(src, dst, load_sem.at[i])
        for i, (src, dst) in enumerate(
            ((key_hbm, key_v), (value_hbm, value_v), (filt_hbm, filt_v), (gate_hbm, gate_v))
        )
    ]
    for load in loads:
        load.start()

    barrier = pltpu.get_barrier_semaphore()

    @pl.loop(1, n)
    def _(off):
        pl.semaphore_signal(
            barrier, inc=1, device_id={"ctx": lax.rem(me + off, n)}, device_id_type=MESH
        )

    pl.semaphore_signal(barrier, inc=1, device_id={"section": after}, device_id_type=MESH)
    pl.semaphore_signal(barrier, inc=1, device_id={"section": before}, device_id_type=MESH)

    @pl.loop(0, n)
    def _(p):
        for h in range(halves):
            got_rows[h, p] = jnp.zeros(got_rows.shape[2:], got_rows.dtype)

    loads[2].wait()
    for h in range(halves):
        block = filt_v[:, h * LANES:(h + 1) * LANES].astype(jnp.float32).T
        taps_send[h] = block.reshape(n, per, 1, LANES)
    loads[0].wait()
    loads[1].wait()

    def rows_copy(h, peer, slot):
        return pltpu.make_async_remote_copy(
            src_ref=send_rows.at[h, peer], dst_ref=got_rows.at[h, n + slot],
            send_sem=rows_ssem.at[h, peer], recv_sem=rows_rsem.at[h, slot],
            device_id={"ctx": peer}, device_id_type=MESH,
        )

    def taps_copy(peer, slot):
        return pltpu.make_async_remote_copy(
            src_ref=taps_send.at[:, peer], dst_ref=got_taps.at[slot],
            send_sem=taps_ssem.at[peer], recv_sem=taps_rsem.at[slot],
            device_id={"ctx": peer}, device_id_type=MESH,
        )

    def back_copy(h, peer, slot):
        return pltpu.make_async_remote_copy(
            src_ref=conv_send.at[h, peer], dst_ref=conv_got.at[h, slot],
            send_sem=back_ssem.at[h, peer], recv_sem=back_rsem.at[h, slot],
            device_id={"ctx": peer}, device_id_type=MESH,
        )

    def pass_copy(h, k):
        cols = pl.ds(k * groups + h * LANES, LANES)
        return pltpu.make_async_remote_copy(
            src_ref=gated.at[:, cols], dst_ref=out_hbm.at[:, cols],
            send_sem=pass_ssem.at[h, k], recv_sem=pass_rsem.at[h, k],
            device_id={"section": after}, device_id_type=MESH,
        )

    def mixed_of(h, k):
        cols = slice(k * groups + h * LANES, k * groups + (h + 1) * LANES)
        product = key_v[:, cols].astype(jnp.float32) * value_v[:, cols].astype(jnp.float32)
        return product.astype(jnp.bfloat16).astype(jnp.float32)

    def peers(body):
        @pl.loop(1, n)
        def _(off):
            body(lax.rem(me + off, n))

    own_taps = pltpu.make_async_copy(taps_send.at[:, me], got_taps.at[me], own_sem.at[0])
    own_rows = [
        pltpu.make_async_copy(send_rows.at[h, me], got_rows.at[h, n + me], own_sem.at[1 + h])
        for h in range(halves)
    ]
    own_back = [
        pltpu.make_async_copy(conv_send.at[h, me], conv_got.at[h, me], own_sem.at[1 + halves + h])
        for h in range(halves)
    ]

    for h in range(halves):
        for k in range(depth):
            turned[pl.ds(k, LANES, stride=depth), :] = mixed_of(h, k).T
        send_rows[h] = turned[...].astype(jnp.bfloat16).reshape(n, per, depth, rows)
        if h == 0:
            pl.semaphore_wait(barrier, n + 1)
            peers(lambda peer: taps_copy(peer, me).start())
            own_taps.start()
        peers(lambda peer: rows_copy(h, peer, me).start())
        own_rows[h].start()

    lane = lax.broadcasted_iota(jnp.int32, (rows, rows), 1)
    line = lax.broadcasted_iota(jnp.int32, (rows, rows), 0)
    upper = lane >= line

    def spread(row):
        return pltpu.roll(
            jnp.broadcast_to(row, (rows, rows)), 0, 1, stride=1, stride_axis=0
        )

    for h in range(halves):
        if h == 0:
            own_taps.wait()
            peers(lambda peer: taps_copy(me, peer).wait_recv())
        own_rows[h].wait()
        peers(lambda peer: rows_copy(h, me, peer).wait_recv())

        @pl.loop(0, per)
        def _(f):
            def piece(first, prev_row):
                prev = None if prev_row is None else spread(prev_row)
                blocks = []
                lhs = []
                for i in range(taps):
                    now = spread(got_taps[first + i, h, f])
                    low = jnp.zeros_like(now) if prev is None else prev
                    blocks.append(jnp.where(upper, now, low).astype(jnp.bfloat16))
                    prev = now
                    lhs.append(
                        got_rows[h, pl.ds(n - first - i, n), f].reshape(n * depth, rows)
                    )
                return jnp.dot(
                    jnp.concatenate(lhs, axis=1), jnp.concatenate(blocks, axis=0),
                    preferred_element_type=jnp.float32,
                )

            total = piece(0, None)
            if n > taps:
                acc_ref[...] = total

                @pl.loop(1, n // taps)
                def _(step):
                    first = step * taps
                    acc_ref[...] += piece(first, got_taps[first - 1, h, f])

                total = acc_ref[...]
            conv_send[h, :, f] = total.astype(jnp.bfloat16).reshape(n, depth, rows)

        peers(lambda peer: back_copy(h, peer, me).start())
        own_back[h].start()

    loads[3].wait()
    for h in range(halves):
        own_back[h].wait()
        peers(lambda peer: back_copy(h, me, peer).wait_recv())
        turned[...] = conv_got[h].reshape(LANES * depth, rows).astype(jnp.float32)
        for k in range(depth):
            cols = slice(k * groups + h * LANES, k * groups + (h + 1) * LANES)
            convolved = turned[pl.ds(k, LANES, stride=depth), :].T
            gated[:, cols] = (
                gate_v[:, cols].astype(jnp.float32)
                * (convolved + skip_ref[:, cols] * mixed_of(h, k))
            ).astype(jnp.bfloat16)
            pass_copy(h, k).start()

    for h in range(halves):
        for k in range(depth):
            pass_copy(h, k).wait()
    peers(lambda peer: taps_copy(peer, me).wait_send())
    for h in range(halves):
        peers(lambda peer: rows_copy(h, peer, me).wait_send())
        peers(lambda peer: back_copy(h, peer, me).wait_send())


def local(gate_rows, key_rows, value_rows, filters, skip_gain):
    n = lax.axis_size("ctx")
    sections = lax.axis_size("section")
    rows, channels = gate_rows.shape[1:]
    groups = filters.shape[2]
    depth = channels // groups
    halves = groups // LANES
    per = LANES // n
    bf16, f32 = jnp.bfloat16, jnp.float32
    hbm = pl.BlockSpec(memory_space=pl.ANY)
    dma = pltpu.SemaphoreType.DMA
    taps = min(n, 8)
    out = pl.pallas_call(
        functools.partial(kernel, n, sections, taps),
        out_shape=jax.ShapeDtypeStruct((rows, channels), bf16),
        in_specs=[hbm] * 4 + [pl.BlockSpec(memory_space=pltpu.VMEM)],
        out_specs=hbm,
        scratch_shapes=[
            pltpu.VMEM((rows, channels), bf16),
            pltpu.VMEM((rows, channels), bf16),
            pltpu.VMEM((rows, channels), bf16),
            pltpu.VMEM((rows, groups), bf16),
            pltpu.VMEM((LANES * depth, rows), f32),
            pltpu.VMEM((halves, n, per, depth, rows), bf16),
            pltpu.VMEM((halves, n, per, 1, rows), f32),
            pltpu.VMEM((halves, 2 * n, per, depth, rows), bf16),
            pltpu.VMEM((n, halves, per, 1, rows), f32),
            pltpu.VMEM((halves, n, per, depth, rows), bf16),
            pltpu.VMEM((halves, n, per, depth, rows), bf16),
            pltpu.VMEM((rows, channels), bf16),
            pltpu.VMEM((n * depth, rows), f32),
            dma((4,)),
            dma((halves, n)), dma((halves, n)),
            dma((n,)), dma((n,)),
            dma((halves, n)), dma((halves, n)),
            dma((halves, depth)), dma((halves, depth)),
            dma((1 + 2 * halves,)),
        ],
        compiler_params=pltpu.CompilerParams(
            collective_id=0, has_side_effects=True, vmem_limit_bytes=40 * 2**20
        ),
    )(gate_rows[0], key_rows[0], value_rows[0], filters[0], skip_gain[None])
    return out[None]


def solution(mesh):
    rows = P("section", "ctx", None)
    return jax.shard_map(
        local, mesh=mesh, in_specs=(rows, rows, rows, rows, P()), out_specs=rows,
        check_vma=False,
    )
```

profile of v0, /device:TPU:0, one launch (start us, length us, event | category | flops | bytes accessed | tf_op | source)
XLA Modules:
  0.0 60.0 jit_solution(7777837855849234618)
XLA Ops:
  0.0 0.0 copy-start
  0.0 1.2 %copy-done = bf16[1,128,4096]{2,1,0:T(8,128)(2,1)S(1)} copy-done((bf16[1,128,4096]{2,1,0:T(8,128)(2,1)S(1)}, bf16[1,128,4096]{2,1,0:T(8,128)(2,1)}, u32[]{:S(2)}) %copy-start) | copy-done | bytes 1048600
  1.2 0.0 copy-start.1
  1.2 1.2 %copy-done.1 = bf16[1,128,4096]{2,1,0:T(8,128)(2,1)S(1)} copy-done((bf16[1,128,4096]{2,1,0:T(8,128)(2,1)S(1)}, bf16[1,128,4096]{2,1,0:T(8,128)(2,1)}, u32[]{:S(2)}) %copy-start.1) | copy-done | bytes 1048600
  2.5 0.0 copy-start.2
  2.5 1.2 %copy-done.2 = bf16[1,128,4096]{2,1,0:T(8,128)(2,1)S(1)} copy-done((bf16[1,128,4096]{2,1,0:T(8,128)(2,1)S(1)}, bf16[1,128,4096]{2,1,0:T(8,128)(2,1)}, u32[]{:S(2)}) %copy-start.2) | copy-done | bytes 1048600
  3.7 0.0 copy-start.3
  3.7 0.8 %copy-done.3 = bf16[1,128,256]{2,1,0:T(8,128)(2,1)S(1)} copy-done((bf16[1,128,256]{2,1,0:T(8,128)(2,1)S(1)}, bf16[1,128,256]{2,1,0:T(8,128)(2,1)}, u32[]{:S(2)}) %copy-start.3) | copy-done | bytes 65560
  4.5 0.0 copy-start.4
  4.5 0.7 %copy-done.4 = f32[4096]{0:T(1024)S(1)} copy-done((f32[4096]{0:T(1024)S(1)}, f32[4096]{0:T(1024)}, u32[]{:S(2)}) %copy-start.4) | copy-done | bytes 16408
  5.2 53.7 %shard_map.55 = bf16[128,4096]{1,0:T(8,128)(2,1)S(1)} custom-call(bf16[128,4096]{1,0:T(8,128)(2,1)S(1)} %bitcast.7, bf16[128,4096]{1,0:T(8,128)(2,1)S(1)} %bitcast.8, bf16[128,4096]{1,0:T(8,128)(2,1)S(1)} %bitcast.9, bf16[128,256]{1,0:T(8,128)(2,1)S(1)} %bitcast.10, f32[1,4096]{1,0:T(1,128)S(1)} %bitcast.11), custom_call_target="tpu_custom_call" | custom-call | tf_op jit(solution)/shard_map/pallas_call | solution.py:209
  59.0 1.0 %copy.7 = bf16[1,128,4096]{2,1,0:T(8,128)(2,1)} copy(bf16[1,128,4096]{2,1,0:T(8,128)(2,1)S(1)} %bitcast.6) | data formatting | bytes 2097152
Async XLA Ops:
  0.0 1.2 %copy-start = (bf16[1,128,4096]{2,1,0:T(8,128)(2,1)S(1)}, bf16[1,128,4096]{2,1,0:T(8,128)(2,1)}, u32[]{:S(2)}) copy-start(bf16[1,128,4096]{2,1,0:T(8,128)(2,1)} %param.5) | copy-start | bytes 3145732
  1.2 1.2 %copy-start.1 = (bf16[1,128,4096]{2,1,0:T(8,128)(2,1)S(1)}, bf16[1,128,4096]{2,1,0:T(8,128)(2,1)}, u32[]{:S(2)}) copy-start(bf16[1,128,4096]{2,1,0:T(8,128)(2,1)} %param.6) | copy-start | bytes 3145732
  2.5 1.2 %copy-start.2 = (bf16[1,128,4096]{2,1,0:T(8,128)(2,1)S(1)}, bf16[1,128,4096]{2,1,0:T(8,128)(2,1)}, u32[]{:S(2)}) copy-start(bf16[1,128,4096]{2,1,0:T(8,128)(2,1)} %param.7) | copy-start | bytes 3145732
  3.7 0.8 %copy-start.3 = (bf16[1,128,256]{2,1,0:T(8,128)(2,1)S(1)}, bf16[1,128,256]{2,1,0:T(8,128)(2,1)}, u32[]{:S(2)}) copy-start(bf16[1,128,256]{2,1,0:T(8,128)(2,1)} %param.8) | copy-start | bytes 196612
  4.5 0.7 %copy-start.4 = (f32[4096]{0:T(1024)S(1)}, f32[4096]{0:T(1024)}, u32[]{:S(2)}) copy-start(f32[4096]{0:T(1024)} %param.9) | copy-start | bytes 49156
where the time goes:
time: 60.3 us; the launch traced here: 60 us
  Pallas kernels  53.7 us (89%)
  local copies, waits for them, and re-layouts  6.2 us (10%)
    pallas_call x1, Pallas kernels, local(): pl.pallas_call(functools.partial(kernel, n, sections, taps), out_shape=ja...  53.7 us
    unnamed x11, local copies, waits for them, and re-layouts  6.2 us

commit v1 on v0

v1 whole, which is shorter than its diff:
```python
import functools

import jax
import jax.numpy as jnp
from jax import lax
from jax.experimental import pallas as pl
from jax.experimental.pallas import tpu as pltpu
from jax.sharding import PartitionSpec as P

MESH = pl.DeviceIdType.MESH
LANES = 128


def kernel(
    n, sections, pack, parts,
    gate_hbm, key_hbm, value_hbm, filt_hbm, skip_ref, out_hbm,
    gate_v, key_v, value_v, filt_v, turned, send_rows, taps_send, got_rows, got_taps,
    conv_send, conv_got, gated, tiles, acc_ref, skips,
    load_sem, rows_ssem, rows_rsem, taps_ssem, taps_rsem,
    back_ssem, back_rsem, pass_ssem, pass_rsem, own_sem,
):
    rows = key_v.shape[0]
    groups = filt_v.shape[1]
    depth = key_v.shape[1] // groups
    halves = groups // LANES
    per = LANES // n
    span = depth // pack
    sets = per // pack
    sub = sets // parts
    chunks = [(h, s) for h in range(halves) for s in range(pack)]
    taps = min(n, 8)
    me = lax.axis_index("ctx")
    sec = lax.axis_index("section")
    after = lax.rem(sec + 1, sections)
    before = lax.rem(sec + sections - 1, sections)

    loads = [
        pltpu.make_async_copy(src, dst, load_sem.at[i])
        for i, (src, dst) in enumerate(
            ((filt_hbm, filt_v), (key_hbm, key_v), (value_hbm, value_v), (gate_hbm, gate_v))
        )
    ]
    for load in loads:
        load.start()

    barrier = pltpu.get_barrier_semaphore()
    pl.semaphore_signal(barrier, inc=1, device_id={"section": before}, device_id_type=MESH)

    @pl.loop(1, n)
    def _(off):
        pl.semaphore_signal(
            barrier, inc=1, device_id={"ctx": lax.rem(me + off, n)}, device_id_type=MESH
        )

    @pl.loop(0, n)
    def _(p):
        for c in range(len(chunks)):
            got_rows[c, p] = jnp.zeros(got_rows.shape[2:], got_rows.dtype)

    for k in range(depth):
        skips[k:k + 1, :] = skip_ref[:, k * groups:(k + 1) * groups]

    def rows_copy(c, j, peer, slot):
        part = pl.ds(j * sub, sub)
        return pltpu.make_async_remote_copy(
            src_ref=send_rows.at[c, peer, part], dst_ref=got_rows.at[c, n + slot, part],
            send_sem=rows_ssem.at[c, j, peer], recv_sem=rows_rsem.at[c, j, slot],
            device_id={"ctx": peer}, device_id_type=MESH,
        )

    def taps_copy(h, peer, slot):
        return pltpu.make_async_remote_copy(
            src_ref=taps_send.at[h, peer], dst_ref=got_taps.at[h, slot],
            send_sem=taps_ssem.at[h, peer], recv_sem=taps_rsem.at[h, slot],
            device_id={"ctx": peer}, device_id_type=MESH,
        )

    def back_copy(c, j, peer, slot):
        part = pl.ds(j * sub, sub)
        return pltpu.make_async_remote_copy(
            src_ref=conv_send.at[c, peer, part], dst_ref=conv_got.at[c, slot, part],
            send_sem=back_ssem.at[c, j, peer], recv_sem=back_rsem.at[c, j, slot],
            device_id={"ctx": peer}, device_id_type=MESH,
        )

    def pass_copy(h, k):
        cols = pl.ds(k * groups + h * LANES, LANES)
        return pltpu.make_async_remote_copy(
            src_ref=gated.at[:, cols], dst_ref=out_hbm.at[:, cols],
            send_sem=pass_ssem.at[h, k], recv_sem=pass_rsem.at[h, k],
            device_id={"section": after}, device_id_type=MESH,
        )

    def own_taps(h):
        return pltpu.make_async_copy(taps_send.at[h, me], got_taps.at[h, me], own_sem.at[0, h])

    def own_rows(c):
        return pltpu.make_async_copy(
            send_rows.at[c, me], got_rows.at[c, n + me], own_sem.at[1, c]
        )

    def own_back(c):
        return pltpu.make_async_copy(conv_send.at[c, me], conv_got.at[c, me], own_sem.at[2, c])

    def others(body):
        @pl.loop(1, n)
        def _(off):
            body(lax.rem(me + off, n))

    def turn(c):
        h, s = chunks[c]
        for i in range(span):
            first = (s * span + i) * groups + h * LANES
            cols = slice(first, first + LANES)
            product = key_v[:, cols].astype(jnp.float32) * value_v[:, cols].astype(jnp.float32)
            product = product.astype(jnp.bfloat16).astype(jnp.float32)
            turned[pl.ds(i, LANES, stride=span), :] = product.T
        send_rows[c] = turned[...].astype(jnp.bfloat16).reshape(n, sets, pack * span, rows)

    def send(c):
        for j in range(parts):
            others(lambda peer: rows_copy(c, j, peer, me).start())
        own_rows(c).start()

    loads[0].wait()
    for h in range(halves):
        block = filt_v[:, h * LANES:(h + 1) * LANES].astype(jnp.float32).T
        taps_send[h] = block.reshape(n, per, 1, LANES)
    loads[1].wait()
    loads[2].wait()
    turn(0)
    pl.semaphore_wait(barrier, n)
    others(lambda peer: taps_copy(0, peer, me).start())
    own_taps(0).start()
    send(0)
    for h in range(1, halves):
        others(lambda peer: taps_copy(h, peer, me).start())
        own_taps(h).start()
    for c in range(1, pack):
        turn(c)
        send(c)

    lane = lax.broadcasted_iota(jnp.int32, (rows, rows), 1)
    line = lax.broadcasted_iota(jnp.int32, (rows, rows), 0)
    upper = lane >= line
    slot_lane = lax.broadcasted_iota(jnp.int32, (depth, LANES), 1)

    def spread(row):
        return pltpu.roll(
            jnp.broadcast_to(row, (rows, rows)), 0, 1, stride=1, stride_axis=0
        )

    def build(h):
        own_taps(h).wait()
        others(lambda peer: taps_copy(h, me, peer).wait_recv())

        @pl.loop(0, sets)
        def _(g):
            for a in range(pack):
                f = g * pack + a

                def stretch(first, prev):
                    for i in range(taps):
                        now = spread(got_taps[h, first + i, f])
                        low = jnp.zeros_like(now) if prev is None else prev
                        tiles[h, g, first + i, :, a * LANES:(a + 1) * LANES] = jnp.where(
                            upper, now, low
                        ).astype(jnp.bfloat16)
                        prev = now

                stretch(0, None)
                if n > taps:
                    @pl.loop(1, n // taps)
                    def _(step):
                        stretch(step * taps, spread(got_taps[h, step * taps - 1, f]))

    def convolve(c):
        h, s = chunks[c]
        own_rows(c).wait()

        def one(g):
            def piece(first):
                lhs = [
                    got_rows[c, pl.ds(n - first - i, n), g].reshape(n * pack * span, rows)
                    for i in range(taps)
                ]
                weights = tiles[h, g, pl.ds(first, taps)].reshape(taps * rows, pack * LANES)
                return jnp.dot(
                    jnp.concatenate(lhs, axis=1), weights,
                    preferred_element_type=jnp.float32,
                )

            total = piece(0)
            if n > taps:
                acc_ref[...] = total

                @pl.loop(1, n // taps)
                def _(step):
                    acc_ref[...] += piece(step * taps)

                total = acc_ref[...]
            total = total.reshape(n, pack, span, pack * LANES)
            own = got_rows[c, n:, g].astype(jnp.float32).reshape(n, pack, span, rows)
            gains = skips[:, h * LANES:(h + 1) * LANES]
            done = []
            for a in range(pack):
                gain = jnp.sum(
                    jnp.where(slot_lane == me * per + g * pack + a, gains, 0.0),
                    axis=1, keepdims=True,
                )[s * span:(s + 1) * span]
                done.append(
                    total[:, a, :, a * LANES:(a + 1) * LANES] + gain[None] * own[:, a]
                )
            conv_send[c, :, g] = jnp.concatenate(done, axis=1).astype(jnp.bfloat16)

        for j in range(parts):
            others(lambda peer: rows_copy(c, j, me, peer).wait_recv())
            pl.loop(j * sub, (j + 1) * sub)(one)
            others(lambda peer: back_copy(c, j, peer, me).start())
        own_back(c).start()

    def finish(c):
        h, s = chunks[c]
        own_back(c).wait()
        for j in range(parts):
            others(lambda peer: back_copy(c, j, me, peer).wait_recv())
        turned[...] = conv_got[c].reshape(LANES * span, rows).astype(jnp.float32)
        for i in range(span):
            k = s * span + i
            cols = slice(k * groups + h * LANES, k * groups + (h + 1) * LANES)
            convolved = turned[pl.ds(i, LANES, stride=span), :].T
            gated[:, cols] = (gate_v[:, cols].astype(jnp.float32) * convolved).astype(
                jnp.bfloat16
            )
            pass_copy(h, k).start()

    build(0)
    for c in range(pack):
        convolve(c)
    for c in range(pack, len(chunks)):
        turn(c)
        send(c)
    loads[3].wait()
    finish(0)
    for h in range(1, halves):
        build(h)
    for c in range(1, pack):
        finish(c)
    for c in range(pack, len(chunks)):
        convolve(c)
    for c in range(pack, len(chunks)):
        finish(c)

    for h in range(halves):
        for k in range(depth):
            pass_copy(h, k).wait()
        others(lambda peer: taps_copy(h, peer, me).wait_send())
    for c in range(len(chunks)):
        for j in range(parts):
            others(lambda peer: rows_copy(c, j, peer, me).wait_send())
            others(lambda peer: back_copy(c, j, peer, me).wait_send())


def local(gate_rows, key_rows, value_rows, filters, skip_gain):
    n = lax.axis_size("ctx")
    sections = lax.axis_size("section")
    rows, channels = gate_rows.shape[1:]
    groups = filters.shape[2]
    depth = channels // groups
    halves = groups // LANES
    per = LANES // n
    bf16, f32 = jnp.bfloat16, jnp.float32
    hbm = pl.BlockSpec(memory_space=pltpu.HBM)
    dma = pltpu.SemaphoreType.DMA
    pack = 2 if per % 2 == 0 and depth % 16 == 0 else 1
    span, sets, chunks = depth // pack, per // pack, halves * pack
    parts = 2 if sets % 2 == 0 else 1
    out = pl.pallas_call(
        functools.partial(kernel, n, sections, pack, parts),
        out_shape=jax.ShapeDtypeStruct((rows, channels), bf16),
        in_specs=[hbm] * 4 + [pl.BlockSpec(memory_space=pltpu.VMEM)],
        out_specs=hbm,
        scratch_shapes=[
            pltpu.VMEM((rows, channels), bf16),
            pltpu.VMEM((rows, channels), bf16),
            pltpu.VMEM((rows, channels), bf16),
            pltpu.VMEM((rows, groups), bf16),
            pltpu.VMEM((LANES * span, rows), f32),
            pltpu.VMEM((chunks, n, sets, depth, rows), bf16),
            pltpu.VMEM((halves, n, per, 1, rows), f32),
            pltpu.VMEM((chunks, 2 * n, sets, depth, rows), bf16),
            pltpu.VMEM((halves, n, per, 1, rows), f32),
            pltpu.VMEM((chunks, n, sets, depth, rows), bf16),
            pltpu.VMEM((chunks, n, sets, depth, rows), bf16),
            pltpu.VMEM((rows, channels), bf16),
            pltpu.VMEM((halves, sets, n, rows, pack * LANES), bf16),
            pltpu.VMEM((n * depth, pack * LANES), f32),
            pltpu.VMEM((depth, groups), f32),
            dma((4,)),
            dma((chunks, parts, n)), dma((chunks, parts, n)),
            dma((halves, n)), dma((halves, n)),
            dma((chunks, parts, n)), dma((chunks, parts, n)),
            dma((halves, depth)), dma((halves, depth)),
            dma((3, chunks)),
        ],
        compiler_params=pltpu.CompilerParams(
            collective_id=0, has_side_effects=True, vmem_limit_bytes=60 * 2**20
        ),
    )(gate_rows[0], key_rows[0], value_rows[0], filters[0], skip_gain[None])
    return out[None]


def solution(mesh):
    rows = P("section", "ctx", None)
    return jax.shard_map(
        local, mesh=mesh, in_specs=(rows, rows, rows, rows, P()), out_specs=rows,
        check_vma=False,
    )
```

time: 60.3 us -> 50.6 us (0.84)
  Pallas kernels: 53.7 us -> 48.1 us
  local copies, waits for them, and re-layouts: 6.2 us -> 2.29 us
    pallas_call x1, Pallas kernels: 53.7 us -> 48.1 us  [local(): pl.pallas_call(functools.partial(kernel, n, sections, pack, parts), out_s...]
    unnamed x11 -> x1, local copies, waits for them, and re-layouts: 6.2 us -> 2.29 us
where the time goes in v1:
time: 50.6 us; the launch traced here: 50.4 us
  Pallas kernels  48.1 us (95%)
  local copies, waits for them, and re-layouts  2.29 us (5%)
    pallas_call x1, Pallas kernels, local(): pl.pallas_call(functools.partial(kernel, n, sections, pack, parts), out_s...  48.1 us
    unnamed x1, local copies, waits for them, and re-layouts  2.29 us

profile of v1, /device:TPU:0, one launch (start us, length us, event | category | flops | bytes accessed | tf_op | source)
XLA Modules:
  0.0 50.4 jit_solution(17841421651659411832)
XLA Ops:
  0.0 48.1 %shard_map.55 = bf16[128,4096]{1,0:T(8,128)(2,1)} custom-call(bf16[128,4096]{1,0:T(8,128)(2,1)} %bitcast.7, bf16[128,4096]{1,0:T(8,128)(2,1)} %bitcast.8, bf16[128,4096]{1,0:T(8,128)(2,1)} %bitcast.9, bf16[128,256]{1,0:T(8,128)(2,1)} %bitcast.10, f32[1,4096]{1,0:T(1,128)} %bitcast.11), custom_call_target="tpu_custom_call" | custom-call | tf_op jit(solution)/shard_map/pallas_call | solution.py:278
  48.1 2.3 %copy.7 = bf16[1,128,4096]{2,1,0:T(8,128)(2,1)} copy(bf16[1,128,4096]{2,1,0:T(8,128)(2,1)} %bitcast.6) | data formatting | bytes 2097152
